TPU v7x, 32 devices: a whole 2x2x4 slice. The times are simulated.
32 devices in a mesh: member: 8 (over z, x), tile: 4 (over y, core).
Axes of the slice: x: 2, y: 2, z: 4, core: 2. Of those that a mesh axis runs over, the one named last changes fastest.
Arguments:
- ensemble: bfloat16 [256, 128, 320], P('member', 'tile'), may hold values from -6 to 6
- departures: bfloat16 [128, 128, 256], P(('tile', 'member')), may hold values from -6 to 6
- innovations: float32 [128, 128], P(('tile', 'member')), may hold values from -12 to 12
- precision: float32 [128, 128], P(('tile', 'member')), may hold values from 0.2 to 5
- obs_count: int32 [128], P(('tile', 'member')), may hold values from 16 to 128
- tile_counts: int32 [4], replicated, may hold values from 0 to 32, as said below
Outputs:
- analysis: bfloat16 [256, 128, 320], P('member', 'tile')
Inputs may be any that keep to these rules, and one draw needn't show every extreme that they name: `tile_counts`: each count is a multiple of 8; all counts sum to 64, and for every tile t the counts of tiles 0 to t - 1 sum to t * 8 * 2 plus or minus at most 8.
All inputs are finite; a program needn't handle non-finite values.
Results may differ from a plain program's by a relative error of at most 0.0049.
Values may be sent and summed in bfloat16 or wider, within the bound.
A program may use at most 64 MiB of HBM per device.

v0:
```python
import jax
import jax.numpy as jnp
from jax import lax
from jax.sharding import PartitionSpec as P

WORK = 2
ITERS = 6


HIGHEST = lax.Precision.HIGHEST


def prepare(departures, innovations, precision, obs_count):
    row_ids = jnp.arange(departures.shape[1], dtype=jnp.int32)
    weight = jnp.where(row_ids[None, :] < obs_count[:, None], jnp.sqrt(precision), jnp.float32(0.0))
    scaled = (departures.astype(jnp.float32) * weight[:, :, None]).astype(jnp.bfloat16)
    signal = (weight * innovations).astype(jnp.bfloat16)
    return (scaled, signal)


def analyse(columns, scaled, signal):
    members = columns.shape[0]
    average = jnp.mean(columns.astype(jnp.float32), axis=0)
    spread = (columns.astype(jnp.float32) - average[None]).astype(jnp.bfloat16)
    gram_matrix = jnp.einsum("npk,npj->nkj", scaled, scaled, preferred_element_type=jnp.float32)
    pull_term = jnp.einsum("npk,np->nk", scaled, signal, preferred_element_type=jnp.float32)
    identity = jnp.eye(members, dtype=jnp.float32)
    system = gram_matrix + (members - 1.0) * identity
    scale_norm = jnp.sqrt(jnp.sum(system * system, axis=(1, 2)))
    root_iter = system / scale_norm[:, None, None]
    inverse_iter = jnp.broadcast_to(identity, system.shape)
    for repeat in range(ITERS):
        factor = 1.5 * identity - 0.5 * jnp.einsum(
            "nij,njk->nik", inverse_iter, root_iter, precision=HIGHEST
        )
        if repeat + 1 < ITERS:
            root_iter = jnp.einsum("nij,njk->nik", root_iter, factor, precision=HIGHEST)
        inverse_iter = jnp.einsum("nij,njk->nik", factor, inverse_iter, precision=HIGHEST)
    halfway = jnp.einsum("njk,nk->nj", inverse_iter, pull_term, precision=HIGHEST)
    shift_w = (
        jnp.einsum("njk,nk->nj", inverse_iter, halfway, precision=HIGHEST) / scale_norm[:, None]
    )
    transform = (
        jnp.sqrt((members - 1.0) / scale_norm)[:, None, None] * inverse_iter + shift_w[:, :, None]
    ).astype(jnp.bfloat16)
    update = jnp.einsum("njk,jnv->knv", transform, spread, preferred_element_type=jnp.float32)
    return (average[None] + update).astype(jnp.bfloat16)


def plan_indices(tile_counts, groups, capacity):
    margin = WORK // 2
    per_tile = tile_counts // groups
    tile_ids = jnp.arange(per_tile.shape[0], dtype=jnp.int32)
    before_sum = jnp.cumsum(per_tile) - per_tile
    tile_here = lax.axis_index("tile")
    lead_gap = jnp.take(before_sum - tile_ids * WORK, tile_here)
    trail_gap = jnp.take(before_sum + per_tile - (tile_ids + 1) * WORK, tile_here)
    count_here = jnp.take(per_tile, tile_here)
    positions = jnp.arange(capacity, dtype=jnp.int32)
    is_live = positions < count_here
    margin_ids = jnp.arange(margin, dtype=jnp.int32)
    send_index = jnp.clip(
        jnp.concatenate([margin_ids, WORK - lead_gap + margin_ids]), 0, capacity - 1
    )
    work_ids = jnp.arange(WORK, dtype=jnp.int32)
    take_index = jnp.where(
        work_ids < jnp.maximum(lead_gap, 0),
        capacity + work_ids,
        jnp.where(
            work_ids >= WORK + jnp.minimum(trail_gap, 0),
            capacity + margin + work_ids - WORK - trail_gap,
            work_ids - lead_gap,
        ),
    )
    take_index = jnp.clip(take_index, 0, capacity + 2 * margin - 1)
    return_index = jnp.clip(
        jnp.concatenate([margin_ids, WORK + trail_gap + margin_ids]), 0, WORK - 1
    )
    home_index = jnp.where(
        positions < jnp.maximum(-lead_gap, 0),
        WORK + positions,
        jnp.where(
            positions >= WORK - lead_gap, margin + positions + lead_gap, positions + lead_gap
        ),
    )
    home_index = jnp.clip(home_index, 0, WORK + 2 * margin - 1)
    return (is_live, send_index, take_index, return_index, home_index)


def to_columns(blocked):
    return lax.all_to_all(blocked, "member", split_axis=1, concat_axis=0, tiled=True)


def to_members(finished):
    return lax.all_to_all(finished, "member", split_axis=0, concat_axis=1, tiled=True)


def on_device(ensemble, departures, innovations, precision, obs_count, tile_counts):
    groups = lax.axis_size("member")
    part_rows = ensemble.shape[0]
    column_len = ensemble.shape[2]
    capacity = departures.shape[0]
    members = departures.shape[2]
    scaled, signal = prepare(departures, innovations, precision, obs_count)
    is_live, send_index, take_index, return_index, home_index = plan_indices(
        tile_counts, groups, capacity
    )
    blocked = ensemble.reshape(part_rows, groups, capacity, column_len)
    columns = to_columns(blocked).reshape(members, capacity, column_len)
    result = analyse(columns, scaled, signal)
    result = jnp.where(is_live[None, :, None], result, columns)
    return to_members(result)


def solution(mesh):
    placed = (
        P("member", "tile", None),
        P(("tile", "member"), None, None),
        P(("tile", "member"), None),
        P(("tile", "member"), None),
        P(("tile", "member")),
        P(),
    )
    return jax.shard_map(
        on_device, mesh=mesh, in_specs=placed, out_specs=P("member", "tile", None), check_vma=False
    )
```

profile of v0, /device:TPU:0, one launch (start us, length us, event | category | flops | bytes accessed | tf_op | source)
XLA Modules:
  0.0 62.8 jit_solution(8051921909998657316)
XLA Ops:
  0.0 2.3 %copy.22 = bf16[32,32,320]{2,0,1:T(8,128)(2,1)} copy(bf16[32,32,320]{2,1,0:T(8,128)(2,1)} %param.6) | data formatting | bytes 1310720 | tf_op args[0]
  2.3 7.4 %all-to-all-start = ((bf16[32,8,4,320]{3,0,2,1:T(8,128)(2,1)}), bf16[32,8,4,320]{3,0,2,1:T(8,128)(2,1)S(1)}, u32[]{:S(2)}, u32[]{:S(2)}) async-start(bf16[32,8,4,320]{3,0,2,1:T(8,128)(2,1)} %bitcast.2), calls=%async_computation | async-start | bytes 1572864 | tf_op jit(solution)/shard_map/all_to_all | solution.py:91
  10.5 1.2 %fusion.5 = f32[4,256,256]{2,1,0:T(8,128)S(1)} fusion(f32[256,256]{1,0:T(8,128)S(1)} %fusion.15, f32[256,256]{1,0:T(8,128)S(1)} %fusion.16, f32[4,256,256]{2,1,0:T(8,128)S(1)} %get-tuple-element.21, f32[4]{0:T(128)S(1)} %get-tuple-element.19), kind=kOutput, calls=%fused_computation.14 | convolution fusion | flops 806092800 | bytes 2621456 | tf_op jit(solution)/shard_map/nij,njk->nik/dot_general | solution.py:33
  11.7 1.2 %fusion.19 = f32[4,256,256]{2,1,0:T(8,128)S(1)} fusion(f32[4,256,256]{2,1,0:T(8,128)S(1)} %fusion.5, f32[4,256,256]{2,1,0:T(8,128)S(1)} %get-tuple-element.21, f32[4]{0:T(128)S(1)} %get-tuple-element.19), kind=kOutput, calls=%fused_computation.34 | convolution fusion | flops 805568512 | bytes 3145744 | tf_op jit(solution)/shard_map/nij,njk->nik/dot_general | solution.py:37
  12.9 1.1 %fusion.11 = f32[4,256,256]{2,1,0:T(8,128)S(1)} fusion(f32[4,256,256]{2,1,0:T(8,128)S(1)} %fusion.5, f32[256,256]{1,0:T(8,128)S(1)} %fusion.15), kind=kOutput, calls=%fused_computation.24 | convolution fusion | flops 805306368 | bytes 2359296 | tf_op jit(solution)/shard_map/nij,njk->nik/dot_general | solution.py:38
  14.0 1.2 %fusion.4 = f32[4,256,256]{2,1,0:T(8,128)S(1)} fusion(f32[4,256,256]{2,1,0:T(8,128)S(1)} %fusion.11, f32[4,256,256]{2,1,0:T(8,128)S(1)} %fusion.19, f32[256,256]{1,0:T(8,128)S(1)} %fusion.16), kind=kOutput, calls=%fused_computation.12 | convolution fusion | flops 805830656 | bytes 3407872 | tf_op jit(solution)/shard_map/nij,njk->nik/dot_general | solution.py:33
  15.2 1.1 %fusion.27 = f32[4,256,256]{2,1,0:T(8,128)S(1)} fusion(f32[4,256,256]{2,1,0:T(8,128)S(1)} %fusion.19, f32[4,256,256]{2,1,0:T(8,128)S(1)} %fusion.4), kind=kOutput, calls=%fused_computation.55 | convolution fusion | flops 805306368 | bytes 3145728 | tf_op jit(solution)/shard_map/nij,njk->nik/dot_general | solution.py:37
  16.3 1.1 %fusion.26 = f32[4,256,256]{2,1,0:T(8,128)S(1)} fusion(f32[4,256,256]{2,1,0:T(8,128)S(1)} %fusion.4, f32[4,256,256]{2,1,0:T(8,128)S(1)} %fusion.11), kind=kOutput, calls=%fused_computation.54 | convolution fusion | flops 805306368 | bytes 3145728 | tf_op jit(solution)/shard_map/nij,njk->nik/dot_general | solution.py:38
  17.5 1.2 %fusion.3 = f32[4,256,256]{2,1,0:T(8,128)S(1)} fusion(f32[4,256,256]{2,1,0:T(8,128)S(1)} %fusion.26, f32[4,256,256]{2,1,0:T(8,128)S(1)} %fusion.27, f32[256,256]{1,0:T(8,128)S(1)} %fusion.16), kind=kOutput, calls=%fused_computation.10 | convolution fusion | flops 805830656 | bytes 3407872 | tf_op jit(solution)/shard_map/nij,njk->nik/dot_general | solution.py:33
  18.7 1.1 %fusion.29 = f32[4,256,256]{2,1,0:T(8,128)S(1)} fusion(f32[4,256,256]{2,1,0:T(8,128)S(1)} %fusion.27, f32[4,256,256]{2,1,0:T(8,128)S(1)} %fusion.3), kind=kOutput, calls=%fused_computation.57 | convolution fusion | flops 805306368 | bytes 3145728 | tf_op jit(solution)/shard_map/nij,njk->nik/dot_general | solution.py:37
  19.8 1.1 %fusion.28 = f32[4,256,256]{2,1,0:T(8,128)S(1)} fusion(f32[4,256,256]{2,1,0:T(8,128)S(1)} %fusion.3, f32[4,256,256]{2,1,0:T(8,128)S(1)} %fusion.26), kind=kOutput, calls=%fused_computation.56 | convolution fusion | flops 805306368 | bytes 3145728 | tf_op jit(solution)/shard_map/nij,njk->nik/dot_general | solution.py:38
  21.0 1.4 %fusion.2 = f32[4,256,256]{2,1,0:T(8,128)S(1)} fusion(f32[4,256,256]{2,1,0:T(8,128)S(1)} %fusion.28, f32[4,256,256]{2,1,0:T(8,128)S(1)} %fusion.29, f32[256,256]{1,0:T(8,128)S(1)} %fusion.16), kind=kOutput, calls=%fused_computation.8 | convolution fusion | flops 805830656 | bytes 3407872 | tf_op jit(solution)/shard_map/nij,njk->nik/dot_general | solution.py:33
  22.4 1.1 %fusion.31 = f32[4,256,256]{2,1,0:T(8,128)S(1)} fusion(f32[4,256,256]{2,1,0:T(8,128)S(1)} %fusion.29, f32[4,256,256]{2,1,0:T(8,128)S(1)} %fusion.2), kind=kOutput, calls=%fused_computation.59 | convolution fusion | flops 805306368 | bytes 3145728 | tf_op jit(solution)/shard_map/nij,njk->nik/dot_general | solution.py:37
  23.5 1.1 %fusion.30 = f32[4,256,256]{2,1,0:T(8,128)S(1)} fusion(f32[4,256,256]{2,1,0:T(8,128)S(1)} %fusion.2, f32[4,256,256]{2,1,0:T(8,128)S(1)} %fusion.28), kind=kOutput, calls=%fused_computation.58 | convolution fusion | flops 805306368 | bytes 3145728 | tf_op jit(solution)/shard_map/nij,njk->nik/dot_general | solution.py:38
  24.7 1.2 %fusion.1 = f32[4,256,256]{2,1,0:T(8,128)S(1)} fusion(f32[4,256,256]{2,1,0:T(8,128)S(1)} %fusion.30, f32[4,256,256]{2,1,0:T(8,128)S(1)} %fusion.31, f32[256,256]{1,0:T(8,128)S(1)} %fusion.16), kind=kOutput, calls=%fused_computation.6 | convolution fusion | flops 805830656 | bytes 3407872 | tf_op jit(solution)/shard_map/nij,njk->nik/dot_general | solution.py:33
  25.9 1.1 %fusion.33 = f32[4,256,256]{2,1,0:T(8,128)S(1)} fusion(f32[4,256,256]{2,1,0:T(8,128)S(1)} %fusion.31, f32[4,256,256]{2,1,0:T(8,128)S(1)} %fusion.1), kind=kOutput, calls=%fused_computation.61 | convolution fusion | flops 805306368 | bytes 3145728 | tf_op jit(solution)/shard_map/nij,njk->nik/dot_general | solution.py:37
  27.1 1.1 %fusion.32 = f32[4,256,256]{2,1,0:T(8,128)S(1)} fusion(f32[4,256,256]{2,1,0:T(8,128)S(1)} %fusion.1, f32[4,256,256]{2,1,0:T(8,128)S(1)} %fusion.30), kind=kOutput, calls=%fused_computation.60 | convolution fusion | flops 805306368 | bytes 3145728 | tf_op jit(solution)/shard_map/nij,njk->nik/dot_general | solution.py:38
  28.2 1.2 %fusion = f32[4,256,256]{2,1,0:T(8,128)S(1)} fusion(f32[4,256,256]{2,1,0:T(8,128)S(1)} %fusion.32, f32[4,256,256]{2,1,0:T(8,128)S(1)} %fusion.33, f32[256,256]{1,0:T(8,128)S(1)} %fusion.16), kind=kOutput, calls=%fused_computation.4 | convolution fusion | flops 805830656 | bytes 3407872 | tf_op jit(solution)/shard_map/nij,njk->nik/dot_general | solution.py:33
  29.4 1.1 %fusion.34 = f32[4,256,256]{2,1,0:T(8,128)S(1)} fusion(f32[4,256,256]{2,1,0:T(8,128)S(1)} %fusion, f32[4,256,256]{2,1,0:T(8,128)S(1)} %fusion.32), kind=kOutput, calls=%fused_computation.62 | convolution fusion | flops 805306368 | bytes 3145728 | tf_op jit(solution)/shard_map/nij,njk->nik/dot_general | solution.py:38
  30.8 1.0 %fusion.22 = f32[4,1,256]{2,1,0:T(1,128)S(1)} fusion(f32[4,256,256]{2,1,0:T(8,128)S(1)} %fusion.34, f32[4,256,1]{1,0,2:T(4,128)S(1)} %bitcast.66), kind=kOutput, calls=%fused_computation.39 | convolution fusion | flops 3145728 | bytes 1056768 | tf_op jit(solution)/shard_map/njk,nk->nj/dot_general | solution.py:39
  33.0 1.0 %fusion.20 = f32[4,1,256]{2,1,0:T(1,128)S(1)} fusion(f32[4,256,256]{2,1,0:T(8,128)S(1)} %fusion.34, f32[4,256,1]{1,0,2:T(4,128)S(1)} %bitcast.65), kind=kOutput, calls=%fused_computation.36 | convolution fusion | flops 3145728 | bytes 1056768 | tf_op jit(solution)/shard_map/njk,nk->nj/dot_general | solution.py:41
  34.6 0.8 %fusion.8 = bf16[256,4,320]{0,2,1:T(8,128)(2,1)S(1)} fusion(bf16[256,4,320]{0,2,1:T(8,128)(2,1)S(1)} %copy.26, bf16[256,4,320]{2,0,1:T(8,128)(2,1)S(1)} %bitcast.64, f32[4,320]{1,0:T(4,128)S(1)} %broadcast_multiply_fusion, pred[4]{0:T(512)(128)(4,1)S(1)} %iota_compare_fusion.2, f32[4,256,256]{2,1,0:T(8,128)S(1)} %fusion.34, ...), kind=kOutput, calls=%fused_computation.18 | convolution fusion | flops 170524672 | bytes 3023892 | tf_op jit(solution)/shard_map/njk,jnv->knv/dot_general | solution.py:46
  36.1 25.4 %all_to_all.33 = bf16[256,4,320]{2,1,0:T(4,128)(2,1)S(1)} all-to-all(bf16[256,4,320]{2,1,0:T(4,128)(2,1)S(1)} %copy.27), channel_id=1, replica_groups=mesh['member'=8,'tile'=4] {'member'}, dimensions={0} | all-to-all | bytes 1310720 | tf_op jit(solution)/shard_map/all_to_all | solution.py:95
  61.7 1.1 %copy.30 = bf16[32,32,320]{2,1,0:T(8,128)(2,1)} copy(bf16[32,32,320]{2,0,1:T(8,128)(2,1)S(1)} %bitcast.62) | data formatting | bytes 1310720 | tf_op jit(solution)/shard_map/all_to_all | solution.py:95
  (31 shorter events, 3.1 us)
Async XLA Ops:
  2.3 7.5 %copy-start.1 = (f32[4,128]{1,0:T(4,128)S(1)}, f32[4,128]{1,0:T(4,128)}, u32[]{:S(2)}) copy-start(f32[4,128]{1,0:T(4,128)} %param.8) | copy-start | bytes 6148
  2.3 7.5 %copy-start.2 = (f32[4,128]{1,0:T(4,128)S(1)}, f32[4,128]{1,0:T(4,128)}, u32[]{:S(2)}) copy-start(f32[4,128]{1,0:T(4,128)} %param.9) | copy-start | bytes 6148
  2.3 7.5 %copy-start.3 = (s32[4]{0:T(128)S(1)}, s32[4]{0:T(128)}, u32[]{:S(2)}) copy-start(s32[4]{0:T(128)} %param.10) | copy-start | bytes 52
  2.3 7.6 %copy-start = (bf16[4,128,256]{2,1,0:T(8,128)(2,1)S(1)}, bf16[4,128,256]{2,1,0:T(8,128)(2,1)}, u32[]{:S(2)}) copy-start(bf16[4,128,256]{2,1,0:T(8,128)(2,1)} %param.7) | copy-start | bytes 786436
  2.3 31.8 %all-to-all-start = ((bf16[32,8,4,320]{3,0,2,1:T(8,128)(2,1)}), bf16[32,8,4,320]{3,0,2,1:T(8,128)(2,1)S(1)}, u32[]{:S(2)}, u32[]{:S(2)}) async-start(bf16[32,8,4,320]{3,0,2,1:T(8,128)(2,1)} %bitcast.2), calls=%async_computation | async-start | bytes 1572864 | tf_op jit(solution)/shard_map/all_to_all | solution.py:91
  30.6 1.3 %copy-start.4 = (s32[4]{0:T(128)S(1)}, s32[4]{0:T(128)}, u32[]{:S(2)}) copy-start(s32[4]{0:T(128)} %param.11) | copy-start | bytes 52
where the time goes:
time: 63.1 us; the launch traced here: 62.8 us
  blocking collectives  25.4 us (40%)
  matrix products  23.5 us (37%)
  starting transfers between devices  7.42 us (12%)
  local copies, waits for them, and re-layouts  5.29 us (8%)
  between operations  0.82 us (1%)
    all_to_all x1, blocking collectives, to_members(): lax.all_to_all(finished, 'member', split_axis=0, concat_axis=1, tiled=True)  25.4 us
    all_to_all x1, starting transfers between devices, to_columns(): lax.all_to_all(blocked, 'member', split_axis=1, concat_axis=0, tiled=True)  7.42 us
    dot_general x6, matrix products, analyse(): jnp.einsum('nij,njk->nik', inverse_iter, root_iter, precision=HIGHEST)  7.3 us
    dot_general x6, matrix products, analyse(): jnp.einsum('nij,njk->nik', factor, inverse_iter, precision=HIGHEST)  6.82 us
    dot_general x5, matrix products, analyse(): root_iter = jnp.einsum('nij,njk->nik', root_iter, factor, precision=HIGHEST)  5.8 us
    unnamed x11, local copies, waits for them, and re-layouts  2.29 us
    all_to_all x3, local copies, waits for them, and re-layouts, to_members(): lax.all_to_all(finished, 'member', split_axis=0, concat_axis=1, tiled=True)  1.34 us
  transfers between devices with their start and end apart: 1, of which 0 were waited for; matrix products, arithmetic and copies ran while one was open for 38% of the time, Pallas kernels for 0%

commit v1 on v0

--- a/solution.py
+++ b/solution.py
@@ -7,7 +7,7 @@
 ITERS = 6
 
 
-HIGHEST = lax.Precision.HIGHEST
+HIGHEST = lax.Precision.HIGH
 
 
 def prepare(departures, innovations, precision, obs_count):
@@ -87,12 +87,18 @@
     return (is_live, send_index, take_index, return_index, home_index)
 
 
-def to_columns(blocked):
-    return lax.all_to_all(blocked, "member", split_axis=1, concat_axis=0, tiled=True)
+def pick(index, slots):
+    picked = slots[-1]
+    for slot in range(len(slots) - 2, -1, -1):
+        picked = jnp.where(index == slot, slots[slot], picked)
+    return picked
 
 
-def to_members(finished):
-    return lax.all_to_all(finished, "member", split_axis=0, concat_axis=1, tiled=True)
+def shift_tiles(to_left, to_right):
+    tiles = lax.axis_size("tile")
+    from_right = lax.ppermute(to_left, "tile", [(t, t - 1) for t in range(1, tiles)])
+    from_left = lax.ppermute(to_right, "tile", [(t, t + 1) for t in range(tiles - 1)])
+    return from_left, from_right
 
 
 def on_device(ensemble, departures, innovations, precision, obs_count, tile_counts):
@@ -105,11 +111,31 @@
     is_live, send_index, take_index, return_index, home_index = plan_indices(
         tile_counts, groups, capacity
     )
-    blocked = ensemble.reshape(part_rows, groups, capacity, column_len)
-    columns = to_columns(blocked).reshape(members, capacity, column_len)
-    result = analyse(columns, scaled, signal)
-    result = jnp.where(is_live[None, :, None], result, columns)
-    return to_members(result)
+
+    def balance(slots):
+        lefts, rights = shift_tiles(pick(send_index[0], slots), pick(send_index[1], slots))
+        every = slots + [lefts, rights]
+        return [pick(take_index[w], every) for w in range(WORK)]
+
+    scaled2 = jnp.stack(balance([scaled[i] for i in range(capacity)]))
+    signal2 = jnp.stack(balance([signal[i] for i in range(capacity)]))
+    blocked = ensemble.reshape(part_rows, groups, capacity, column_len).transpose(2, 1, 0, 3)
+    own = [blocked[i] for i in range(capacity)]
+    work = balance(own)
+    packed = jnp.stack(work, axis=1)
+    columns = lax.all_to_all(packed, "member", split_axis=0, concat_axis=0, tiled=True)
+    columns = columns.transpose(0, 2, 1, 3).reshape(members, WORK, column_len)
+    result = analyse(columns, scaled2, signal2)
+    result = result.reshape(groups, part_rows, WORK, column_len).transpose(0, 2, 1, 3)
+    back = lax.all_to_all(result, "member", split_axis=0, concat_axis=0, tiled=True)
+    home = [back[:, w] for w in range(WORK)]
+    lefts, rights = shift_tiles(pick(return_index[0], home), pick(return_index[1], home))
+    every = home + [lefts, rights]
+    outs = [
+        jnp.where(is_live[i], pick(home_index[i], every), own[i]) for i in range(capacity)
+    ]
+    out = jnp.stack(outs, axis=0).transpose(2, 1, 0, 3)
+    return out.reshape(part_rows, groups * capacity, column_len)
 
 
 def solution(mesh):

time: 63.1 us -> 97.2 us (1.54)
  blocking collectives: 25.4 us -> 0 us
  starting transfers between devices: 7.42 us -> 30.5 us
  between operations: 0.82 us -> 21.9 us
  waiting for transfers between devices: 0.01 us -> 19.4 us
  matrix products: 23.5 us -> 8.24 us
  other arithmetic: 0.38 us -> 7.18 us
  local copies, waits for them, and re-layouts: 5.29 us -> 8.98 us
    all_to_all x1 -> x0, blocking collectives: 25.4 us -> none  [to_members(): lax.all_to_all(finished, 'member', split_axis=0, concat_axis=1, tiled=True)]
    ppermute x0 -> x8, starting transfers between devices: none -> 20.7 us  [the longest x4 15.5 us: shift_tiles(): lax.ppermute(to_right, 'tile', [(t, t + 1) for t in range(tiles - 1)])]
    all_to_all x1 -> x2, waiting for transfers between devices: 0.01 us -> 19.4 us  [the longest x1 11.9 us: on_device(): lax.all_to_all(packed, 'member', split_axis=0, concat_axis=0, tiled=True)]
    dot_general x6, matrix products: 7.3 us -> 2.42 us  [analyse(): jnp.einsum('nij,njk->nik', inverse_iter, root_iter, precision=HIGHEST)]
    dot_general x6, matrix products: 6.82 us -> 2.31 us  [analyse(): jnp.einsum('nij,njk->nik', factor, inverse_iter, precision=HIGHEST)]
    dot_general x5, matrix products: 5.8 us -> 1.95 us  [analyse(): root_iter = jnp.einsum('nij,njk->nik', root_iter, factor, precision=HIGHEST)]
    another operation x0 -> x12, other arithmetic: none -> 3.84 us  [the longest x2 2.64 us: on_device(): out = jnp.stack(outs, axis=0).transpose(2, 1, 0, 3)]
    slice x0 -> x5, local copies, waits for them, and re-layouts: none -> 3.17 us  [the longest x1 0.66 us: on_device(): home_index[i]]
  transfers between devices with their start and end apart: 1 -> 10, of which waited for: 0 -> 2; matrix products, arithmetic and copies ran while one was open for 38% -> 13% of each run, Pallas kernels for 0% -> 0%
where the time goes in v1:
time: 97.2 us; the launch traced here: 96.3 us
  starting transfers between devices  30.5 us (31%)
  between operations  21.9 us (23%)
  waiting for transfers between devices  19.4 us (20%)
  local copies, waits for them, and re-layouts  8.98 us (9%)
  matrix products  8.24 us (8%)
  other arithmetic  7.18 us (7%)
    ppermute x4, starting transfers between devices, shift_tiles(): lax.ppermute(to_right, 'tile', [(t, t + 1) for t in range(tiles - 1)])  15.5 us
    all_to_all x1, waiting for transfers between devices, on_device(): lax.all_to_all(packed, 'member', split_axis=0, concat_axis=0, tiled=True)  11.9 us
    all_to_all x1, waiting for transfers between devices, on_device(): lax.all_to_all(result, 'member', split_axis=0, concat_axis=0, tiled=True)  7.52 us
    all_to_all x1, starting transfers between devices, on_device(): lax.all_to_all(packed, 'member', split_axis=0, concat_axis=0, tiled=True)  5.8 us
    ppermute x4, starting transfers between devices, shift_tiles(): lax.ppermute(to_left, 'tile', [(t, t - 1) for t in range(1, tiles)])  5.17 us
    all_to_all x1, starting transfers between devices, on_device(): lax.all_to_all(result, 'member', split_axis=0, concat_axis=0, tiled=True)  4.08 us
    another operation x2, other arithmetic, on_device(): out = jnp.stack(outs, axis=0).transpose(2, 1, 0, 3)  2.64 us
    dot_general x6, matrix products, analyse(): jnp.einsum('nij,njk->nik', inverse_iter, root_iter, precision=HIGHEST)  2.42 us
  transfers between devices with their start and end apart: 10, of which 2 were waited for; matrix products, arithmetic and copies ran while one was open for 13% of the time, Pallas kernels for 0%

profile of v1, /device:TPU:0, one launch (start us, length us, event | category | flops | bytes accessed | tf_op | source)
XLA Modules:
  0.0 96.3 jit_solution(7321267040905557335)
XLA Ops:
  0.0 0.7 fusion.80
  0.9 0.7 fusion.30
  8.7 0.8 multiply_convert_fusion.1
  9.5 1.3 %collective-permute-start.5 = (bf16[128]{0:T(256)(128)(2,1)S(1)}, bf16[128]{0:T(256)(128)(2,1)S(1)}, u32[]{:S(2)}, u32[]{:S(2)}) collective-permute-start(bf16[128]{0:T(256)(128)(2,1)S(1)} %get-tuple-element.50), channel_id=1, source_target_pairs={{1,0},{2,1},{3,2},{5,4},{6,5},{7,6},{9,8},{10,9},{11,10},{13,12},{... | collective-permute-start | bytes 776 | tf_op jit(solution)/shard_map/ppermute | solution.py:99
  10.8 3.0 %collective-permute-start.4 = (bf16[128]{0:T(256)(128)(2,1)S(1)}, bf16[128]{0:T(256)(128)(2,1)S(1)}, u32[]{:S(2)}, u32[]{:S(2)}) collective-permute-start(bf16[128]{0:T(256)(128)(2,1)S(1)} %get-tuple-element.51), channel_id=1, source_target_pairs={{0,1},{1,2},{2,3},{4,5},{5,6},{6,7},{8,9},{9,10},{10,11},{12,13},{... | collective-permute-start | bytes 776 | tf_op jit(solution)/shard_map/ppermute | solution.py:100
  13.9 1.1 %multiply_convert_fusion = bf16[4,128,256]{2,1,0:T(8,128)(2,1)S(1)} fusion(bf16[4,128,256]{2,1,0:T(8,128)(2,1)} %param.7, f32[4,128]{1,0:T(4,128)S(1)} %get-tuple-element.39), kind=kLoop, calls=%fused_computation.23 | loop fusion | flops 393216 | bytes 526336 | tf_op jit(solution)/shard_map/convert_element_type | solution.py:16
  15.0 1.3 %collective-permute-start.3 = (bf16[128,256]{1,0:T(8,128)(2,1)S(1)}, bf16[128,256]{1,0:T(8,128)(2,1)S(1)}, u32[]{:S(2)}, u32[]{:S(2)}) collective-permute-start(bf16[128,256]{1,0:T(8,128)(2,1)S(1)} %get-tuple-element.48), channel_id=1, source_target_pairs={{1,0},{2,1},{3,2},{5,4},{6,5},{7,6},{9,8},{10,9},{11,10},{13,12},{... | collective-permute-start | bytes 196616 | tf_op jit(solution)/shard_map/ppermute | solution.py:99
  16.3 5.2 %collective-permute-start.2 = (bf16[128,256]{1,0:T(8,128)(2,1)S(1)}, bf16[128,256]{1,0:T(8,128)(2,1)S(1)}, u32[]{:S(2)}, u32[]{:S(2)}) collective-permute-start(bf16[128,256]{1,0:T(8,128)(2,1)S(1)} %get-tuple-element.49), channel_id=1, source_target_pairs={{0,1},{1,2},{2,3},{4,5},{5,6},{6,7},{8,9},{9,10},{10,11},{12,13},{... | collective-permute-start | bytes 196616 | tf_op jit(solution)/shard_map/ppermute | solution.py:100
  21.8 1.3 %collective-permute-start.1 = (bf16[8,32,320]{2,1,0:T(8,128)(2,1)S(1)}, bf16[8,32,320]{2,1,0:T(8,128)(2,1)S(1)}, u32[]{:S(2)}, u32[]{:S(2)}) collective-permute-start(bf16[8,32,320]{2,1,0:T(8,128)(2,1)S(1)} %get-tuple-element.44), channel_id=1, source_target_pairs={{1,0},{2,1},{3,2},{5,4},{6,5},{7,6},{9,8},{10,9},{11,10},{13,12},{... | collective-permute-start | bytes 491528 | tf_op jit(solution)/shard_map/ppermute | solution.py:99
  30.2 4.3 %collective-permute-start = (bf16[8,32,320]{2,1,0:T(8,128)(2,1)S(1)}, bf16[8,32,320]{2,1,0:T(8,128)(2,1)S(1)}, u32[]{:S(2)}, u32[]{:S(2)}) collective-permute-start(bf16[8,32,320]{2,1,0:T(8,128)(2,1)S(1)} %get-tuple-element.45), channel_id=1, source_target_pairs={{0,1},{1,2},{2,3},{4,5},{5,6},{6,7},{8,9},{9,10},{10,11},{12,13},{... | collective-permute-start | bytes 491528 | tf_op jit(solution)/shard_map/ppermute | solution.py:100
  42.2 0.8 copy.26
  43.0 5.8 %all-to-all-start = ((bf16[8,2,32,320]{3,2,1,0:T(8,128)(2,1)}), bf16[8,2,32,320]{3,2,1,0:T(8,128)(2,1)S(1)}, u32[]{:S(2)}, u32[]{:S(2)}) async-start(bf16[8,2,32,320]{3,2,1,0:T(8,128)(2,1)} %copy.26), calls=%async_computation | async-start | bytes 786432 | tf_op jit(solution)/shard_map/all_to_all | solution.py:126
  49.6 11.9 %all-to-all-done = bf16[8,2,32,320]{3,2,1,0:T(8,128)(2,1)S(1)} async-done(((bf16[8,2,32,320]{3,2,1,0:T(8,128)(2,1)}), bf16[8,2,32,320]{3,2,1,0:T(8,128)(2,1)S(1)}, u32[]{:S(2)}, u32[]{:S(2)}) %all-to-all-start) | async-done | bytes 327712 | tf_op jit(solution)/shard_map/all_to_all | solution.py:126
  62.4 0.8 copy.31
  63.2 4.1 %all-to-all-start.1 = ((bf16[8,2,32,320]{3,2,1,0:T(8,128)(2,1)}), bf16[8,2,32,320]{3,2,1,0:T(8,128)(2,1)S(1)}, u32[]{:S(2)}, u32[]{:S(2)}) async-start(bf16[8,2,32,320]{3,2,1,0:T(8,128)(2,1)} %copy.31), calls=%async_computation.1 | async-start | bytes 786432 | tf_op jit(solution)/shard_map/all_to_all | solution.py:130
  67.3 0.7 copy-done.1
  71.1 0.7 fusion.34
  71.7 7.5 %all-to-all-done.1 = bf16[8,2,32,320]{3,2,1,0:T(8,128)(2,1)S(1)} async-done(((bf16[8,2,32,320]{3,2,1,0:T(8,128)(2,1)}), bf16[8,2,32,320]{3,2,1,0:T(8,128)(2,1)S(1)}, u32[]{:S(2)}, u32[]{:S(2)}) %all-to-all-start.1) | async-done | bytes 327712 | tf_op jit(solution)/shard_map/all_to_all | solution.py:130
  79.3 1.3 %collective-permute-start.7 = (bf16[8,32,320]{2,1,0:T(8,128)(2,1)S(1)}, bf16[8,32,320]{2,1,0:T(8,128)(2,1)S(1)}, u32[]{:S(2)}, u32[]{:S(2)}) collective-permute-start(bf16[8,32,320]{2,1,0:T(8,128)(2,1)S(1)} %get-tuple-element.46), channel_id=1, source_target_pairs={{1,0},{2,1},{3,2},{5,4},{6,5},{7,6},{9,8},{10,9},{11,10},{13,12},{... | collective-permute-start | bytes 491528 | tf_op jit(solution)/shard_map/ppermute | solution.py:99
  80.6 3.0 %collective-permute-start.6 = (bf16[8,32,320]{2,1,0:T(8,128)(2,1)S(1)}, bf16[8,32,320]{2,1,0:T(8,128)(2,1)S(1)}, u32[]{:S(2)}, u32[]{:S(2)}) collective-permute-start(bf16[8,32,320]{2,1,0:T(8,128)(2,1)S(1)} %get-tuple-element.47), channel_id=1, source_target_pairs={{0,1},{1,2},{2,3},{4,5},{5,6},{6,7},{8,9},{9,10},{10,11},{12,13},{... | collective-permute-start | bytes 491528 | tf_op jit(solution)/shard_map/ppermute | solution.py:100
  91.5 0.7 fusion.33
  92.2 1.2 %select_bitcast_fusion.2 = (bf16[1,8,32,320]{3,2,1,0:T(8,128)(2,1)S(1)}, bf16[1,8,32,320]{3,2,1,0:T(8,128)(2,1)S(1)}) fusion(bf16[8,32,320]{2,1,0:T(8,128)(2,1)S(1)} %collective-permute-done.6, bf16[8,32,320]{2,1,0:T(8,128)(2,1)S(1)} %collective-permute-done.7, pred[]{:T(512)} %bitcast.68, pred[]{:T(512)} %bitcast.67, pred[]{:T(512)} %bitcast.66, ...), kind=kLoop, calls=%fused_computation.43 | loop fusion | flops 655360 | bytes 1310728 | tf_op jit(solution)/shard_map/stack | solution.py:137
  93.4 1.4 %select_bitcast_fusion.3 = (bf16[1,8,32,320]{3,2,1,0:T(8,128)(2,1)S(1)}, bf16[1,8,32,320]{3,2,1,0:T(8,128)(2,1)S(1)}) fusion(bf16[8,32,320]{2,1,0:T(8,128)(2,1)S(1)} %collective-permute-done.6, bf16[8,32,320]{2,1,0:T(8,128)(2,1)S(1)} %collective-permute-done.7, pred[]{:T(512)} %bitcast.60, pred[]{:T(512)} %bitcast.58, pred[]{:T(512)} %bitcast.6, ...), kind=kLoop, calls=%fused_computation.44 | loop fusion | flops 655360 | bytes 1310728 | tf_op jit(solution)/shard_map/stack | solution.py:137
  95.1 1.1 %copy.35 = bf16[32,32,320]{2,1,0:T(8,128)(2,1)} copy(bf16[32,32,320]{2,0,1:T(8,128)(2,1)S(1)} %bitcast.280) | data formatting | bytes 1310720 | tf_op jit(solution)/shard_map/reshape | solution.py:138
  (73 shorter events, 13.8 us)
Async XLA Ops:
  0.0 21.5 %copy-start = (bf16[32,32,320]{2,1,0:T(8,128)(2,1)S(1)}, bf16[32,32,320]{2,1,0:T(8,128)(2,1)}, u32[]{:S(2)}) copy-start(bf16[32,32,320]{2,1,0:T(8,128)(2,1)} %param.6) | copy-start | bytes 1966084
  9.5 20.7 %collective-permute-start.5 = (bf16[128]{0:T(256)(128)(2,1)S(1)}, bf16[128]{0:T(256)(128)(2,1)S(1)}, u32[]{:S(2)}, u32[]{:S(2)}) collective-permute-start(bf16[128]{0:T(256)(128)(2,1)S(1)} %get-tuple-element.50), channel_id=1, source_target_pairs={{1,0},{2,1},{3,2},{5,4},{6,5},{7,6},{9,8},{10,9},{11,10},{13,12},{... | collective-permute-start | bytes 776 | tf_op jit(solution)/shard_map/ppermute | solution.py:99
  10.8 23.7 %collective-permute-start.4 = (bf16[128]{0:T(256)(128)(2,1)S(1)}, bf16[128]{0:T(256)(128)(2,1)S(1)}, u32[]{:S(2)}, u32[]{:S(2)}) collective-permute-start(bf16[128]{0:T(256)(128)(2,1)S(1)} %get-tuple-element.51), channel_id=1, source_target_pairs={{0,1},{1,2},{2,3},{4,5},{5,6},{6,7},{8,9},{9,10},{10,11},{12,13},{... | collective-permute-start | bytes 776 | tf_op jit(solution)/shard_map/ppermute | solution.py:100
  15.0 19.6 %collective-permute-start.3 = (bf16[128,256]{1,0:T(8,128)(2,1)S(1)}, bf16[128,256]{1,0:T(8,128)(2,1)S(1)}, u32[]{:S(2)}, u32[]{:S(2)}) collective-permute-start(bf16[128,256]{1,0:T(8,128)(2,1)S(1)} %get-tuple-element.48), channel_id=1, source_target_pairs={{1,0},{2,1},{3,2},{5,4},{6,5},{7,6},{9,8},{10,9},{11,10},{13,12},{... | collective-permute-start | bytes 196616 | tf_op jit(solution)/shard_map/ppermute | solution.py:99
  16.3 18.3 %collective-permute-start.2 = (bf16[128,256]{1,0:T(8,128)(2,1)S(1)}, bf16[128,256]{1,0:T(8,128)(2,1)S(1)}, u32[]{:S(2)}, u32[]{:S(2)}) collective-permute-start(bf16[128,256]{1,0:T(8,128)(2,1)S(1)} %get-tuple-element.49), channel_id=1, source_target_pairs={{0,1},{1,2},{2,3},{4,5},{5,6},{6,7},{8,9},{9,10},{10,11},{12,13},{... | collective-permute-start | bytes 196616 | tf_op jit(solution)/shard_map/ppermute | solution.py:100
  21.8 20.2 %collective-permute-start.1 = (bf16[8,32,320]{2,1,0:T(8,128)(2,1)S(1)}, bf16[8,32,320]{2,1,0:T(8,128)(2,1)S(1)}, u32[]{:S(2)}, u32[]{:S(2)}) collective-permute-start(bf16[8,32,320]{2,1,0:T(8,128)(2,1)S(1)} %get-tuple-element.44), channel_id=1, source_target_pairs={{1,0},{2,1},{3,2},{5,4},{6,5},{7,6},{9,8},{10,9},{11,10},{13,12},{... | collective-permute-start | bytes 491528 | tf_op jit(solution)/shard_map/ppermute | solution.py:99
  30.2 11.8 %collective-permute-start = (bf16[8,32,320]{2,1,0:T(8,128)(2,1)S(1)}, bf16[8,32,320]{2,1,0:T(8,128)(2,1)S(1)}, u32[]{:S(2)}, u32[]{:S(2)}) collective-permute-start(bf16[8,32,320]{2,1,0:T(8,128)(2,1)S(1)} %get-tuple-element.45), channel_id=1, source_target_pairs={{0,1},{1,2},{2,3},{4,5},{5,6},{6,7},{8,9},{9,10},{10,11},{12,13},{... | collective-permute-start | bytes 491528 | tf_op jit(solution)/shard_map/ppermute | solution.py:100
  43.0 18.4 %all-to-all-start = ((bf16[8,2,32,320]{3,2,1,0:T(8,128)(2,1)}), bf16[8,2,32,320]{3,2,1,0:T(8,128)(2,1)S(1)}, u32[]{:S(2)}, u32[]{:S(2)}) async-start(bf16[8,2,32,320]{3,2,1,0:T(8,128)(2,1)} %copy.26), calls=%async_computation | async-start | bytes 786432 | tf_op jit(solution)/shard_map/all_to_all | solution.py:126
  63.2 16.0 %all-to-all-start.1 = ((bf16[8,2,32,320]{3,2,1,0:T(8,128)(2,1)}), bf16[8,2,32,320]{3,2,1,0:T(8,128)(2,1)S(1)}, u32[]{:S(2)}, u32[]{:S(2)}) async-start(bf16[8,2,32,320]{3,2,1,0:T(8,128)(2,1)} %copy.31), calls=%async_computation.1 | async-start | bytes 786432 | tf_op jit(solution)/shard_map/all_to_all | solution.py:130
  67.3 0.7 copy-start.1
  79.3 12.9 %collective-permute-start.7 = (bf16[8,32,320]{2,1,0:T(8,128)(2,1)S(1)}, bf16[8,32,320]{2,1,0:T(8,128)(2,1)S(1)}, u32[]{:S(2)}, u32[]{:S(2)}) collective-permute-start(bf16[8,32,320]{2,1,0:T(8,128)(2,1)S(1)} %get-tuple-element.46), channel_id=1, source_target_pairs={{1,0},{2,1},{3,2},{5,4},{6,5},{7,6},{9,8},{10,9},{11,10},{13,12},{... | collective-permute-start | bytes 491528 | tf_op jit(solution)/shard_map/ppermute | solution.py:99
  80.6 11.6 %collective-permute-start.6 = (bf16[8,32,320]{2,1,0:T(8,128)(2,1)S(1)}, bf16[8,32,320]{2,1,0:T(8,128)(2,1)S(1)}, u32[]{:S(2)}, u32[]{:S(2)}) collective-permute-start(bf16[8,32,320]{2,1,0:T(8,128)(2,1)S(1)} %get-tuple-element.47), channel_id=1, source_target_pairs={{0,1},{1,2},{2,3},{4,5},{5,6},{6,7},{8,9},{9,10},{10,11},{12,13},{... | collective-permute-start | bytes 491528 | tf_op jit(solution)/shard_map/ppermute | solution.py:100

commit v2 on v0

v2 whole, which is shorter than its diff:
```python
import functools

import jax
import jax.numpy as jnp
from jax import lax
from jax.experimental import pallas as pl
from jax.experimental.pallas import tpu as pltpu
from jax.sharding import PartitionSpec as P

WORK = 2
ITERS = 6
SLOTS = WORK + 2
PASSES = (1, 1, 1, 3, 3)
MESH = pl.DeviceIdType.MESH
F32 = jnp.float32
BF16 = jnp.bfloat16


def dot(a, b, ca=1, cb=0):
    return lax.dot_general(a, b, (((ca,), (cb,)), ((), ())), preferred_element_type=F32)


def split(x):
    high = x.astype(BF16)
    return high, (x - high.astype(F32)).astype(BF16)


def mm(a, b, passes):
    if passes == 1:
        return dot(a.astype(BF16), b.astype(BF16))
    ah, al = split(a)
    bh, bl = split(b)
    return dot(ah, bh) + (dot(ah, bl) + dot(al, bh))


def mm_exact(a, b):
    ah, al = split(a)
    return dot(ah, b) + dot(al, b)


def log2(n):
    return n.bit_length() - 1


def kernel(
    tiles, groups, counts_ref, obs_ref, ens_ref, dep_ref, inn_ref, prec_ref, out_ref,
    work, mrg_send, mrg_recv, obs_send, obs_recv, cols, ret, home,
    mrg_ssem, mrg_rsem, obs_ssem, obs_rsem, in_ssem, in_rsem, out_ssem, out_rsem, fwd_ssem, fwd_rsem,
):
    me = lax.axis_index("member")
    tile = lax.axis_index("tile")
    rows, width, length = ens_ref.shape
    capacity, obs_rows, members = dep_ref.shape
    has_left = tile > 0
    has_right = tile < tiles - 1

    barrier = pltpu.get_barrier_semaphore()
    for step in range(1, groups):
        peer = lax.rem(me + step, groups)
        pl.semaphore_signal(barrier, inc=1, device_id=(peer, tile), device_id_type=MESH)

    @pl.when(has_left)
    def _():
        pl.semaphore_signal(barrier, inc=1, device_id=(me, tile - 1), device_id_type=MESH)

    @pl.when(has_right)
    def _():
        pl.semaphore_signal(barrier, inc=1, device_id=(me, tile + 1), device_id_type=MESH)

    before = 0
    here = 0
    for other in range(tiles):
        count = counts_ref[other]
        before = before + jnp.where(other < tile, count, 0)
        here = here + jnp.where(other == tile, count, 0)
    before = before // groups
    here = here // groups
    lead = before - tile * WORK
    trail = before + here - (tile + 1) * WORK
    top = capacity - 1
    own = [jnp.clip(w - lead, 0, top) for w in range(WORK)]
    send_right = jnp.clip(WORK - lead, 0, top)
    from_left = lead > 0
    from_right = trail < 0

    eye_obs = lax.broadcasted_iota(jnp.int32, (obs_rows, obs_rows), 0) == lax.broadcasted_iota(
        jnp.int32, (obs_rows, obs_rows), 1
    )
    row_ids = lax.broadcasted_iota(jnp.int32, (1, obs_rows), 1)

    def observe(index):
        weight = jnp.where(row_ids < obs_ref[index], jnp.sqrt(prec_ref[pl.ds(index, 1), :]), 0.0)
        signal = weight * inn_ref[pl.ds(index, 1), :]
        weight_col = jnp.sum(jnp.where(eye_obs, weight, 0.0), axis=1, keepdims=True)
        scaled = dep_ref[index].astype(F32) * weight_col
        return scaled, jnp.broadcast_to(signal, (16, obs_rows))

    for side, index in enumerate((0, send_right)):
        scaled, signal = observe(index)
        obs_send[side, :obs_rows, :] = scaled.astype(BF16)
        obs_send[side, obs_rows:, :] = jnp.zeros((16, members), BF16)
        obs_send[side, obs_rows:, :obs_rows] = signal.astype(BF16)

    chunk = min(16, rows)
    lc, lg, lw, lcap = log2(chunk), log2(groups), log2(width), log2(capacity)
    block = groups * chunk
    out_row = lax.broadcasted_iota(jnp.int32, (SLOTS * block, 1), 0)
    slot = out_row >> (lc + lg)
    column = jnp.where(
        slot == 0, own[0], jnp.where(slot == 1, own[1], jnp.where(slot == 2, 0, send_right))
    )
    wanted = (
        ((out_row & (chunk - 1)) << lw) + (((out_row >> lc) & (groups - 1)) << lcap) + column
    )
    in_row = lax.broadcasted_iota(jnp.int32, (SLOTS * block, chunk * width), 1)
    gather = jnp.where(in_row == wanted, 1.0, 0.0).astype(BF16)
    for part in range(rows // chunk):
        span = pl.ds(part * chunk, chunk)
        states = ens_ref[span].reshape(chunk * width, length)
        picked = dot(gather, states)
        for s in range(SLOTS):
            piece = picked[s * block:(s + 1) * block].reshape(groups, chunk, length).astype(BF16)
            if s < WORK:
                work[:, s, span, :] = piece
            else:
                mrg_send[s - WORK, :, span, :] = piece

    @pl.when(jnp.logical_not(has_left))
    def _():
        mrg_recv[0] = jnp.zeros(mrg_recv.shape[1:], BF16)
        obs_recv[0] = jnp.zeros(obs_recv.shape[1:], BF16)
        home[WORK] = jnp.zeros(home.shape[1:], BF16)

    @pl.when(jnp.logical_not(has_right))
    def _():
        mrg_recv[1] = jnp.zeros(mrg_recv.shape[1:], BF16)
        obs_recv[1] = jnp.zeros(obs_recv.shape[1:], BF16)
        home[WORK + 1] = jnp.zeros(home.shape[1:], BF16)

    pl.semaphore_wait(
        barrier, groups - 1 + jnp.where(has_left, 1, 0) + jnp.where(has_right, 1, 0)
    )

    def remote(src, dst, ssem, rsem, device):
        return pltpu.make_async_remote_copy(
            src_ref=src, dst_ref=dst, send_sem=ssem, recv_sem=rsem,
            device_id=device, device_id_type=MESH,
        )

    def towards(side):
        return (me, tile - 1) if side == 0 else (me, tile + 1)

    sides = ((0, has_left, has_right), (1, has_right, has_left))

    def obs_copy(side):
        return remote(
            obs_send.at[side], obs_recv.at[1 - side], obs_ssem.at[side], obs_rsem.at[1 - side],
            towards(side),
        )

    def mrg_copy(side):
        return remote(
            mrg_send.at[side], mrg_recv.at[1 - side], mrg_ssem.at[side], mrg_rsem.at[1 - side],
            towards(side),
        )

    for side, sends, _ in sides:

        @pl.when(sends)
        def _(side=side):
            obs_copy(side).start()
            mrg_copy(side).start()

    ours = [observe(own[w]) for w in range(WORK)]

    for side, _, receives in sides:

        @pl.when(receives)
        def _(side=side):
            obs_copy(side).wait_recv()

    takes = (from_left, from_right)
    scaled, signal = [], []
    for w in range(WORK):
        took = jnp.where(takes[w], obs_recv[w, :obs_rows, :].astype(F32), ours[w][0])
        scaled.append(took.astype(BF16))
        took = jnp.where(takes[w], obs_recv[w, obs_rows:, :obs_rows].astype(F32), ours[w][1])
        signal.append(took.astype(BF16))

    for side, _, receives in sides:

        @pl.when(receives)
        def _(side=side):
            mrg_copy(side).wait_recv()

    for w in range(WORK):
        for g in range(groups):
            work[g, w] = jnp.where(
                takes[w], mrg_recv[w, g].astype(F32), work[g, w].astype(F32)
            ).astype(BF16)

    def in_copy(peer, source):
        return remote(
            work.at[peer], cols.at[source], in_ssem.at[peer], in_rsem.at[source], (peer, tile)
        )

    for step in range(1, groups):
        in_copy(lax.rem(me + step, groups), me).start()
    cols[me] = work[me]

    base = members - 1.0
    eye = jnp.where(eye_obs, 1.0, 0.0)
    both = range(WORK)
    gram = [dot(scaled[w], scaled[w], 1, 1) for w in both]
    norm, x, xc, pc, q, p = [], [], [], [], [], []
    for w in both:
        total = jnp.sum(
            gram[w] * gram[w] + (2.0 * base) * jnp.where(eye_obs, gram[w], 0.0), keepdims=True
        )
        norm.append(jnp.sqrt(total + base * base * members))
        x.append(gram[w] / norm[w])
        xc.append(base / norm[w])
        pc.append(1.5 - 0.5 * xc[w])
        q.append(-0.5 * eye)
        p.append(pc[w] * eye - 0.5 * x[w])
    for repeat in range(ITERS - 1):
        n_pass = PASSES[repeat]
        square = [mm(p[w], p[w], n_pass) for w in both]
        mixed = [
            mm(
                jnp.concatenate(
                    [square[w], square[w] + pc[w] * p[w] + (pc[w] * pc[w]) * eye], axis=1
                ),
                jnp.concatenate([p[w], xc[w] * q[w]], axis=0),
                n_pass,
            )
            for w in both
        ]
        for w in both:
            q[w] = 1.5 * q[w] - 0.5 * mixed[w]
            pc[w] = pc[w] * (1.5 - 0.5 * xc[w] * pc[w] * pc[w])
        if repeat + 2 < ITERS:
            p = [pc[w] * eye + mm(x[w], q[w], n_pass) for w in both]

    shift = []
    y = [signal[w].astype(F32) for w in both]
    for _ in range(2):
        y = [pc[w] * y[w] + mm(mm(y[w], q[w], 3), x[w], 3) for w in both]
    for w in both:
        shift.append(mm_exact(y[w], scaled[w])[:1] / norm[w])
    eye_all = lax.broadcasted_iota(jnp.int32, (members, members), 0) == lax.broadcasted_iota(
        jnp.int32, (members, members), 1
    )
    transform = []
    for w in both:
        half = mm_exact(q[w] / norm[w], scaled[w])
        hh, hl = split(half)
        inverse = dot(scaled[w], hh, 0, 0) + dot(scaled[w], hl, 0, 0)
        inverse = inverse + jnp.where(eye_all, pc[w], 0.0)
        transform.append((jnp.sqrt(base / norm[w]) * inverse + shift[w]).astype(BF16))

    for step in range(1, groups):
        in_copy(me, lax.rem(me + step, groups)).wait_recv()

    def out_copy(w, peer, source):
        return remote(
            ret.at[w, peer], home.at[w, source], out_ssem.at[w, peer], out_rsem.at[w, source],
            (peer, tile),
        )

    def fwd_copy(w, source):
        return remote(
            home.at[w, source], home.at[WORK + 1 - w, source],
            fwd_ssem.at[w, source], fwd_rsem.at[1 - w, source], towards(w),
        )

    for w in both:
        states = cols[:, w].astype(F32).reshape(members, length)
        average = jnp.sum(states, axis=0, keepdims=True) * (1.0 / members)
        spread = (states - average).astype(BF16)
        result = average + dot(transform[w], spread)
        ret[w] = result.reshape(groups, rows, length).astype(BF16)
        for step in range(1, groups):
            out_copy(w, lax.rem(me + step, groups), me).start()
        home[w, me] = ret[w, me]

    for step in range(groups):
        source = lax.rem(me + step, groups)
        for w, sends, _ in sides:
            if step:
                out_copy(w, me, source).wait_recv()

            @pl.when(sends)
            def _(w=w, source=source):
                fwd_copy(w, source).start()

    back_row = lax.broadcasted_iota(jnp.int32, (chunk * width, 1), 0)
    position = back_row & (capacity - 1)
    where_to = jnp.where(
        position < jnp.maximum(-lead, 0),
        WORK,
        jnp.where(position >= WORK - lead, WORK + 1, position + lead),
    )
    live = position < here
    target = (
        (where_to << (lc + lg))
        + (((back_row >> lcap) & (groups - 1)) << lc)
        + (back_row >> lw)
    )
    target = jnp.where(live, target, -1)
    home_row = lax.broadcasted_iota(jnp.int32, (chunk * width, SLOTS * block), 1)
    scatter = jnp.where(home_row == target, 1.0, 0.0).astype(BF16)

    for source in range(groups):
        for w, _, receives in sides:

            @pl.when(receives)
            def _(w=w, source=source):
                fwd_copy(w, source).wait_recv()

    for part in range(rows // chunk):
        span = pl.ds(part * chunk, chunk)
        parts = home[:, :, span, :].astype(F32).reshape(SLOTS * block, length).astype(BF16)
        placed = dot(scatter, parts)
        kept = ens_ref[span].reshape(chunk * width, length).astype(F32)
        placed = jnp.where(live, placed, kept)
        out_ref[span] = placed.astype(BF16).reshape(chunk, width, length)

    for side, sends, _ in sides:

        @pl.when(sends)
        def _(side=side):
            obs_copy(side).wait_send()
            mrg_copy(side).wait_send()
            for source in range(groups):
                fwd_copy(side, source).wait_send()

    for step in range(1, groups):
        peer = lax.rem(me + step, groups)
        in_copy(peer, me).wait_send()
        for w in both:
            out_copy(w, peer, me).wait_send()


def on_device(ensemble, departures, innovations, precision, obs_count, tile_counts):
    groups = lax.axis_size("member")
    tiles = lax.axis_size("tile")
    rows, width, length = ensemble.shape
    capacity, obs_rows, members = departures.shape
    vmem = pl.BlockSpec(memory_space=pltpu.VMEM)
    smem = pl.BlockSpec(memory_space=pltpu.SMEM)
    dma = pltpu.SemaphoreType.DMA
    return pl.pallas_call(
        functools.partial(kernel, tiles, groups),
        out_shape=jax.ShapeDtypeStruct(ensemble.shape, BF16),
        in_specs=[smem, smem, vmem, vmem, vmem, vmem],
        out_specs=vmem,
        scratch_shapes=[
            pltpu.VMEM((groups, WORK, rows, length), BF16),
            pltpu.VMEM((2, groups, rows, length), BF16),
            pltpu.VMEM((2, groups, rows, length), BF16),
            pltpu.VMEM((2, obs_rows + 16, members), BF16),
            pltpu.VMEM((2, obs_rows + 16, members), BF16),
            pltpu.VMEM((groups, WORK, rows, length), BF16),
            pltpu.VMEM((WORK, groups, rows, length), BF16),
            pltpu.VMEM((SLOTS, groups, rows, length), BF16),
            dma((2,)), dma((2,)), dma((2,)), dma((2,)),
            dma((groups,)), dma((groups,)),
            dma((WORK, groups)), dma((WORK, groups)),
            dma((WORK, groups)), dma((WORK, groups)),
        ],
        compiler_params=pltpu.CompilerParams(
            collective_id=0, has_side_effects=True, vmem_limit_bytes=56 * 1024 * 1024
        ),
    )(tile_counts, obs_count, ensemble, departures, innovations, precision)


def solution(mesh):
    placed = (
        P("member", "tile", None),
        P(("tile", "member"), None, None),
        P(("tile", "member"), None),
        P(("tile", "member"), None),
        P(("tile", "member")),
        P(),
    )
    return jax.shard_map(
        on_device, mesh=mesh, in_specs=placed, out_specs=P("member", "tile", None), check_vma=False
    )
```

time: 63.1 us -> 39.6 us (0.63)
  the two profiles are of different devices: /device:TPU:0 before, /device:TPU:17 now
where the time goes in v2:
time: 39.6 us; the launch traced here: 39.4 us
  Pallas kernels  37.3 us (94%)
  local copies, waits for them, and re-layouts  2.09 us (5%)
    pallas_call x1, Pallas kernels, on_device(): pl.pallas_call(functools.partial(kernel, tiles, groups), out_shape=jax.Sh...  37.3 us
    unnamed x1, local copies, waits for them, and re-layouts  2.09 us

profile of v2, /device:TPU:17, one launch (start us, length us, event | category | flops | bytes accessed | tf_op | source)
XLA Modules:
  0.0 39.4 jit_solution(16968551287413999720)
XLA Ops:
  0.0 37.3 %shard_map.64 = bf16[32,32,320]{2,1,0:T(8,128)(2,1)} custom-call(s32[4]{0:T(128)} %counts_ref.1, s32[4]{0:T(128)} %obs_ref.1, bf16[32,32,320]{2,1,0:T(8,128)(2,1)} %ens_ref.1, bf16[4,128,256]{2,1,0:T(8,128)(2,1)} %dep_ref.1, f32[4,128]{1,0:T(4,128)} %inn_ref.1, f32[4,128]{1,0:T(4,128)} %prec_ref.1), custom_call_target="tpu_custom_call" | custom-call | tf_op jit(solution)/shard_map/pallas_call | solution.py:353
  37.3 2.1 %copy.8 = bf16[32,32,320]{2,1,0:T(8,128)(2,1)} copy(bf16[32,32,320]{2,1,0:T(8,128)(2,1)} %shard_map.64) | data formatting | bytes 1310720

commit v3 on v2

--- a/solution.py
+++ b/solution.py
@@ -43,12 +43,21 @@
 
 
 def kernel(
-    tiles, groups, counts_ref, obs_ref, ens_ref, dep_ref, inn_ref, prec_ref, out_ref,
+    tiles, groups, counts_ref, obs_ref, ens_hbm, dep_hbm, inn_hbm, prec_hbm, out_ref,
+    ens_ref, dep_ref, inn_ref, prec_ref, load_sem,
     work, mrg_send, mrg_recv, obs_send, obs_recv, cols, ret, home,
     mrg_ssem, mrg_rsem, obs_ssem, obs_rsem, in_ssem, in_rsem, out_ssem, out_rsem, fwd_ssem, fwd_rsem,
 ):
     me = lax.axis_index("member")
     tile = lax.axis_index("tile")
+    loads = [
+        pltpu.make_async_copy(source, kept, load_sem.at[i])
+        for i, (source, kept) in enumerate(
+            ((inn_hbm, inn_ref), (prec_hbm, prec_ref), (dep_hbm, dep_ref), (ens_hbm, ens_ref))
+        )
+    ]
+    for load in loads:
+        load.start()
     rows, width, length = ens_ref.shape
     capacity, obs_rows, members = dep_ref.shape
     has_left = tile > 0
@@ -95,6 +104,8 @@
         scaled = dep_ref[index].astype(F32) * weight_col
         return scaled, jnp.broadcast_to(signal, (16, obs_rows))
 
+    for load in loads[:3]:
+        load.wait()
     for side, index in enumerate((0, send_right)):
         scaled, signal = observe(index)
         obs_send[side, :obs_rows, :] = scaled.astype(BF16)
@@ -114,6 +125,7 @@
     )
     in_row = lax.broadcasted_iota(jnp.int32, (SLOTS * block, chunk * width), 1)
     gather = jnp.where(in_row == wanted, 1.0, 0.0).astype(BF16)
+    loads[3].wait()
     for part in range(rows // chunk):
         span = pl.ds(part * chunk, chunk)
         states = ens_ref[span].reshape(chunk * width, length)
@@ -204,9 +216,12 @@
             work.at[peer], cols.at[source], in_ssem.at[peer], in_rsem.at[source], (peer, tile)
         )
 
-    for step in range(1, groups):
-        in_copy(lax.rem(me + step, groups), me).start()
-    cols[me] = work[me]
+    @pl.when(me >= 0)
+    def _():
+        for step in range(1, groups):
+            in_copy(lax.rem(me + step, groups), me).start()
+        cols[me] = work[me]
+
 
     base = members - 1.0
     eye = jnp.where(eye_obs, 1.0, 0.0)
@@ -349,13 +364,19 @@
     capacity, obs_rows, members = departures.shape
     vmem = pl.BlockSpec(memory_space=pltpu.VMEM)
     smem = pl.BlockSpec(memory_space=pltpu.SMEM)
+    hbm = pl.BlockSpec(memory_space=pl.ANY)
     dma = pltpu.SemaphoreType.DMA
     return pl.pallas_call(
         functools.partial(kernel, tiles, groups),
         out_shape=jax.ShapeDtypeStruct(ensemble.shape, BF16),
-        in_specs=[smem, smem, vmem, vmem, vmem, vmem],
+        in_specs=[smem, smem, hbm, hbm, hbm, hbm],
         out_specs=vmem,
         scratch_shapes=[
+            pltpu.VMEM(ensemble.shape, BF16),
+            pltpu.VMEM(departures.shape, BF16),
+            pltpu.VMEM(innovations.shape, F32),
+            pltpu.VMEM(precision.shape, F32),
+            dma((4,)),
             pltpu.VMEM((groups, WORK, rows, length), BF16),
             pltpu.VMEM((2, groups, rows, length), BF16),
             pltpu.VMEM((2, groups, rows, length), BF16),

time: 39.6 us -> 35.4 us (0.89)
  Pallas kernels: 37.3 us -> 33.1 us
    pallas_call x1, Pallas kernels: 37.3 us -> 33.1 us  [on_device(): pl.pallas_call(functools.partial(kernel, tiles, groups), out_shape=jax.Sh...]
where the time goes in v3:
time: 35.4 us; the launch traced here: 35.2 us
  Pallas kernels  33.1 us (94%)
  local copies, waits for them, and re-layouts  2.09 us (6%)
    pallas_call x1, Pallas kernels, on_device(): pl.pallas_call(functools.partial(kernel, tiles, groups), out_shape=jax.Sh...  33.1 us
    unnamed x1, local copies, waits for them, and re-layouts  2.09 us

profile of v3, /device:TPU:17, one launch (start us, length us, event | category | flops | bytes accessed | tf_op | source)
XLA Modules:
  0.0 35.2 jit_solution(15113656849321643247)
XLA Ops:
  0.0 33.1 %shard_map.64 = bf16[32,32,320]{2,1,0:T(8,128)(2,1)} custom-call(s32[4]{0:T(128)} %counts_ref.1, s32[4]{0:T(128)} %obs_ref.1, bf16[32,32,320]{2,1,0:T(8,128)(2,1)} %ens_hbm.1, bf16[4,128,256]{2,1,0:T(8,128)(2,1)} %dep_hbm.1, f32[4,128]{1,0:T(4,128)} %inn_hbm.1, f32[4,128]{1,0:T(4,128)} %prec_hbm.1), custom_call_target="tpu_custom_call" | custom-call | tf_op jit(solution)/shard_map/pallas_call | solution.py:369
  33.2 2.1 %copy.8 = bf16[32,32,320]{2,1,0:T(8,128)(2,1)} copy(bf16[32,32,320]{2,1,0:T(8,128)(2,1)} %shard_map.64) | data formatting | bytes 1310720

commit v4 on v3

--- a/solution.py
+++ b/solution.py
@@ -368,7 +368,7 @@
     dma = pltpu.SemaphoreType.DMA
     return pl.pallas_call(
         functools.partial(kernel, tiles, groups),
-        out_shape=jax.ShapeDtypeStruct(ensemble.shape, BF16),
+        out_shape=pltpu.VMEM(ensemble.shape, BF16),
         in_specs=[smem, smem, hbm, hbm, hbm, hbm],
         out_specs=vmem,
         scratch_shapes=[

time: 35.4 us -> 33.4 us (0.944)
  local copies, waits for them, and re-layouts: 2.09 us -> 0.88 us
  Pallas kernels: 33.1 us -> 32.3 us
    unnamed x1, local copies, waits for them, and re-layouts: 2.09 us -> 0.88 us
    pallas_call x1, Pallas kernels: 33.1 us -> 32.3 us  [on_device(): pl.pallas_call(functools.partial(kernel, tiles, groups), out_shape=pltpu....]
where the time goes in v4:
time: 33.4 us; the launch traced here: 33.2 us
  Pallas kernels  32.3 us (97%)
  local copies, waits for them, and re-layouts  0.88 us (3%)
    pallas_call x1, Pallas kernels, on_device(): pl.pallas_call(functools.partial(kernel, tiles, groups), out_shape=pltpu....  32.3 us
    unnamed x1, local copies, waits for them, and re-layouts  0.88 us

profile of v4, /device:TPU:17, one launch (start us, length us, event | category | flops | bytes accessed | tf_op | source)
XLA Modules:
  0.0 33.2 jit_solution(17497989945287324940)
XLA Ops:
  0.0 32.3 %shard_map.64 = bf16[32,32,320]{2,1,0:T(8,128)(2,1)S(1)} custom-call(s32[4]{0:T(128)} %counts_ref.1, s32[4]{0:T(128)} %obs_ref.1, bf16[32,32,320]{2,1,0:T(8,128)(2,1)} %ens_hbm.1, bf16[4,128,256]{2,1,0:T(8,128)(2,1)} %dep_hbm.1, f32[4,128]{1,0:T(4,128)} %inn_hbm.1, f32[4,128]{1,0:T(4,128)} %prec_hbm.1), custom_call_target="tpu_custom_call" | custom-call | tf_op jit(solution)/shard_map/pallas_call | solution.py:369
  32.3 0.9 %copy.8 = bf16[32,32,320]{2,1,0:T(8,128)(2,1)} copy(bf16[32,32,320]{2,1,0:T(8,128)(2,1)S(1)} %shard_map.64) | data formatting | bytes 1310720

commit v5 on v4

--- a/solution.py
+++ b/solution.py
@@ -45,7 +45,7 @@
 def kernel(
     tiles, groups, counts_ref, obs_ref, ens_hbm, dep_hbm, inn_hbm, prec_hbm, out_ref,
     ens_ref, dep_ref, inn_ref, prec_ref, load_sem,
-    work, mrg_send, mrg_recv, obs_send, obs_recv, cols, ret, home,
+    work, mrg_send, mrg_recv, obs_send, obs_recv, cols, ret, home, home_left, home_right,
     mrg_ssem, mrg_rsem, obs_ssem, obs_rsem, in_ssem, in_rsem, out_ssem, out_rsem, fwd_ssem, fwd_rsem,
 ):
     me = lax.axis_index("member")
@@ -60,6 +60,9 @@
         load.start()
     rows, width, length = ens_ref.shape
     capacity, obs_rows, members = dep_ref.shape
+    low = length // 128 * 128
+    high = -(-length // 128) * 128
+    lanes = [pl.ds(w * length, length) for w in range(WORK)]
     has_left = tile > 0
     has_right = tile < tiles - 1
 
@@ -133,7 +136,7 @@
         for s in range(SLOTS):
             piece = picked[s * block:(s + 1) * block].reshape(groups, chunk, length).astype(BF16)
             if s < WORK:
-                work[:, s, span, :] = piece
+                work[:, span, lanes[s]] = piece
             else:
                 mrg_send[s - WORK, :, span, :] = piece
 
@@ -141,13 +144,13 @@
     def _():
         mrg_recv[0] = jnp.zeros(mrg_recv.shape[1:], BF16)
         obs_recv[0] = jnp.zeros(obs_recv.shape[1:], BF16)
-        home[WORK] = jnp.zeros(home.shape[1:], BF16)
+        home_left[...] = jnp.zeros(home_left.shape, BF16)
 
     @pl.when(jnp.logical_not(has_right))
     def _():
         mrg_recv[1] = jnp.zeros(mrg_recv.shape[1:], BF16)
         obs_recv[1] = jnp.zeros(obs_recv.shape[1:], BF16)
-        home[WORK + 1] = jnp.zeros(home.shape[1:], BF16)
+        home_right[...] = jnp.zeros(home_right.shape, BF16)
 
     pl.semaphore_wait(
         barrier, groups - 1 + jnp.where(has_left, 1, 0) + jnp.where(has_right, 1, 0)
@@ -207,8 +210,8 @@
 
     for w in range(WORK):
         for g in range(groups):
-            work[g, w] = jnp.where(
-                takes[w], mrg_recv[w, g].astype(F32), work[g, w].astype(F32)
+            work[g, :, lanes[w]] = jnp.where(
+                takes[w], mrg_recv[w, g].astype(F32), work[g, :, lanes[w]].astype(F32)
             ).astype(BF16)
 
     def in_copy(peer, source):
@@ -277,33 +280,36 @@
     for step in range(1, groups):
         in_copy(me, lax.rem(me + step, groups)).wait_recv()
 
-    def out_copy(w, peer, source):
+    def out_copy(peer, source):
         return remote(
-            ret.at[w, peer], home.at[w, source], out_ssem.at[w, peer], out_rsem.at[w, source],
-            (peer, tile),
+            ret.at[peer], home.at[source], out_ssem.at[peer], out_rsem.at[source], (peer, tile)
         )
 
     def fwd_copy(w, source):
+        span = pl.ds(0, high) if w == 0 else pl.ds(low, 2 * length - low)
         return remote(
-            home.at[w, source], home.at[WORK + 1 - w, source],
+            home.at[source, :, span], (home_right if w == 0 else home_left).at[source],
             fwd_ssem.at[w, source], fwd_rsem.at[1 - w, source], towards(w),
         )
 
     for w in both:
-        states = cols[:, w].astype(F32).reshape(members, length)
+        states = cols[:, :, lanes[w]].astype(F32).reshape(members, length)
         average = jnp.sum(states, axis=0, keepdims=True) * (1.0 / members)
         spread = (states - average).astype(BF16)
         result = average + dot(transform[w], spread)
-        ret[w] = result.reshape(groups, rows, length).astype(BF16)
+        ret[:, :, lanes[w]] = result.reshape(groups, rows, length).astype(BF16)
+
+    @pl.when(me >= 0)
+    def _():
         for step in range(1, groups):
-            out_copy(w, lax.rem(me + step, groups), me).start()
-        home[w, me] = ret[w, me]
+            out_copy(lax.rem(me + step, groups), me).start()
+        home[me] = ret[me]
 
     for step in range(groups):
         source = lax.rem(me + step, groups)
+        if step:
+            out_copy(me, source).wait_recv()
         for w, sends, _ in sides:
-            if step:
-                out_copy(w, me, source).wait_recv()
 
             @pl.when(sends)
             def _(w=w, source=source):
@@ -335,7 +341,12 @@
 
     for part in range(rows // chunk):
         span = pl.ds(part * chunk, chunk)
-        parts = home[:, :, span, :].astype(F32).reshape(SLOTS * block, length).astype(BF16)
+        parts = [home[:, span, lanes[w]] for w in both]
+        parts.append(home_left[:, span, pl.ds(length - low, length)])
+        parts.append(home_right[:, span, pl.ds(0, length)])
+        parts = jnp.concatenate(
+            [x.astype(F32).reshape(block, length).astype(BF16) for x in parts], axis=0
+        )
         placed = dot(scatter, parts)
         kept = ens_ref[span].reshape(chunk * width, length).astype(F32)
         placed = jnp.where(live, placed, kept)
@@ -353,8 +364,7 @@
     for step in range(1, groups):
         peer = lax.rem(me + step, groups)
         in_copy(peer, me).wait_send()
-        for w in both:
-            out_copy(w, peer, me).wait_send()
+        out_copy(peer, me).wait_send()
 
 
 def on_device(ensemble, departures, innovations, precision, obs_count, tile_counts):
@@ -377,17 +387,19 @@
             pltpu.VMEM(innovations.shape, F32),
             pltpu.VMEM(precision.shape, F32),
             dma((4,)),
-            pltpu.VMEM((groups, WORK, rows, length), BF16),
+            pltpu.VMEM((groups, rows, WORK * length), BF16),
             pltpu.VMEM((2, groups, rows, length), BF16),
             pltpu.VMEM((2, groups, rows, length), BF16),
             pltpu.VMEM((2, obs_rows + 16, members), BF16),
             pltpu.VMEM((2, obs_rows + 16, members), BF16),
-            pltpu.VMEM((groups, WORK, rows, length), BF16),
-            pltpu.VMEM((WORK, groups, rows, length), BF16),
-            pltpu.VMEM((SLOTS, groups, rows, length), BF16),
+            pltpu.VMEM((groups, rows, WORK * length), BF16),
+            pltpu.VMEM((groups, rows, WORK * length), BF16),
+            pltpu.VMEM((groups, rows, WORK * length), BF16),
+            pltpu.VMEM((groups, rows, WORK * length - length // 128 * 128), BF16),
+            pltpu.VMEM((groups, rows, -(-length // 128) * 128), BF16),
             dma((2,)), dma((2,)), dma((2,)), dma((2,)),
             dma((groups,)), dma((groups,)),
-            dma((WORK, groups)), dma((WORK, groups)),
+            dma((groups,)), dma((groups,)),
             dma((WORK, groups)), dma((WORK, groups)),
         ],
         compiler_params=pltpu.CompilerParams(

time: 33.4 us -> 30.5 us (0.913)
  Pallas kernels: 32.3 us -> 29.1 us
    pallas_call x1, Pallas kernels: 32.3 us -> 29.1 us  [on_device(): pl.pallas_call(functools.partial(kernel, tiles, groups), out_shape=pltpu....]
where the time goes in v5:
time: 30.5 us; the launch traced here: 30 us
  Pallas kernels  29.1 us (95%)
  local copies, waits for them, and re-layouts  0.88 us (3%)
    pallas_call x1, Pallas kernels, on_device(): pl.pallas_call(functools.partial(kernel, tiles, groups), out_shape=pltpu....  29.1 us
    unnamed x1, local copies, waits for them, and re-layouts  0.88 us

profile of v5, /device:TPU:17, one launch (start us, length us, event | category | flops | bytes accessed | tf_op | source)
XLA Modules:
  0.0 30.0 jit_solution(17646107475458859325)
XLA Ops:
  0.0 29.1 %shard_map.64 = bf16[32,32,320]{2,1,0:T(8,128)(2,1)S(1)} custom-call(s32[4]{0:T(128)} %counts_ref.1, s32[4]{0:T(128)} %obs_ref.1, bf16[32,32,320]{2,1,0:T(8,128)(2,1)} %ens_hbm.1, bf16[4,128,256]{2,1,0:T(8,128)(2,1)} %dep_hbm.1, f32[4,128]{1,0:T(4,128)} %inn_hbm.1, f32[4,128]{1,0:T(4,128)} %prec_hbm.1), custom_call_target="tpu_custom_call" | custom-call | tf_op jit(solution)/shard_map/pallas_call | solution.py:379
  29.1 0.9 %copy.8 = bf16[32,32,320]{2,1,0:T(8,128)(2,1)} copy(bf16[32,32,320]{2,1,0:T(8,128)(2,1)S(1)} %shard_map.64) | data formatting | bytes 1310720
